TPU v7x, 32 devices: a whole 2x2x4 slice. The times are simulated.
32 devices in a mesh: grp: 2 (over x), comp: 16 (over z, y, core).
Axes of the slice: x: 2, y: 2, z: 4, core: 2. Of those that a mesh axis runs over, the one named last changes fastest.
Arguments:
- spectrum: float32 [1152, 96, 128], P(None, ('grp', 'comp')), parts along dimension 1, may hold values from 0.04 to 14, as said below
- sea_mask: int32 [96, 128], P(('grp', 'comp')), parts along dimension 0, may hold values 0 or 1
- ice_mask: int32 [96, 128], P(('grp', 'comp')), parts along dimension 0, may hold values 0 or 1
- wind: float32 [96, 128], P(('grp', 'comp')), parts along dimension 0, may hold values from 0.2 to 1
- source_matrix: bfloat16 [1152, 1152], replicated, may hold values from -0.1875 to 0.1875
Outputs:
- evolved: float32 [1152, 96, 128], P(None, ('grp', 'comp')), parts along dimension 1
There are 2 independent parts, one for each index of `grp`. A program takes and returns all parts, laid end to end along the dimension named above; an argument that names none is the same for every part. Nothing has to cross between parts.
Inputs may be any that keep to these rules, and one draw needn't show every extreme that they name: `spectrum`: positive spectral densities.
All inputs are finite; a program needn't handle non-finite values. No bound on the sum of `sea_mask` or of `ice_mask` on one device may be relied on, other than what follows from the above.
Results may differ from a plain program's by a relative error of at most 0.0014.
Values sent between devices are 32-bit elements; how exact they have to be, the bound alone decides.
A program may use at most 64 MiB of HBM per device.

v0:
```python
import functools

import jax
import jax.numpy as jnp
import numpy as np
from jax import lax
from jax.experimental import pallas as pl
from jax.experimental.pallas import tpu as pltpu
from jax.sharding import PartitionSpec as P

NDIR = 36
NFREQ = 32
K = NDIR * NFREQ
STEPS = 2
SUBSTEPS = 3
SRC_SUB = 3
RATE = 0.5
DAMPING = 0.5

HALF = NDIR // 2
QUARTER = HALF // 2
SIDE = HALF * NFREQ
CHUNKS = 3
PER = HALF // CHUNKS
SPAN = PER * NFREQ
TILE = 288
UP_ROW = (1, 2, 0)
DOWN_ROW = (1, 0, 2)
MESH = pl.DeviceIdType.MESH


def tables(width):
    frequency = np.arange(NFREQ, dtype=np.float64)
    speeds = 0.6 * (0.35 + 0.65 * (NFREQ - 1 - frequency) / (NFREQ - 1))
    angles = 2.0 * np.pi * (np.arange(HALF) + 0.5) / NDIR
    trig = np.concatenate([np.abs(np.cos(angles)), np.abs(np.sin(angles))])
    spread = lambda v: np.broadcast_to(v.astype(np.float32)[:, None], (v.size, width)).copy()
    return spread(speeds), spread(trig)


def strided(d):
    return pl.ds(d, NFREQ, stride=NDIR)


def kernel(size, spec, sea_ref, ice_ref, wind_ref, mat_hbm, speed_ref, trig_ref, out,
           nat, work, south, north, send_up, send_down, sea_south, sea_north, mat, low_mid, low_out,
           total, load_sem, mat_sem, mask_send, mask_recv, up_send, up_recv, down_send, down_recv, out_sem):
    rows, width = spec.shape[0], spec.shape[2]
    me = lax.axis_index("comp")
    has_south, has_north = me > 0, me < size - 1

    loads = [pltpu.make_async_copy(spec.at[r], nat.at[r], load_sem.at[r]) for r in range(rows)]
    for r in UP_ROW:
        loads[r].start()

    barrier = pltpu.get_barrier_semaphore()

    @pl.when(has_south)
    def _():
        pl.semaphore_signal(barrier, inc=1, device_id={"comp": me - 1}, device_id_type=MESH)

    @pl.when(has_north)
    def _():
        pl.semaphore_signal(barrier, inc=1, device_id={"comp": me + 1}, device_id_type=MESH)

    def up_copy(step, p, h):
        part = pl.ds(h * SPAN, SPAN)
        return pltpu.make_async_remote_copy(
            src_ref=send_up.at[step, p, part], dst_ref=south.at[step, p, part],
            send_sem=up_send.at[step, p, h], recv_sem=up_recv.at[step, p, h],
            device_id={"comp": me + 1}, device_id_type=MESH)

    def down_copy(step, p, h):
        part = pl.ds(h * SPAN, SPAN)
        return pltpu.make_async_remote_copy(
            src_ref=send_down.at[step, p, part], dst_ref=north.at[step, p, part],
            send_sem=down_send.at[step, p, h], recv_sem=down_recv.at[step, p, h],
            device_id={"comp": me - 1}, device_id_type=MESH)

    def pack(step, p):
        for d in range(HALF):
            send_up[step, p, pl.ds(d * NFREQ, NFREQ), :] = nat[UP_ROW[p], strided(d), :]
            send_down[step, p, pl.ds(d * NFREQ, NFREQ), :] = nat[DOWN_ROW[p], strided(d + HALF), :]

    def send(step, p):
        @pl.when(has_north)
        def _():
            for h in range(CHUNKS):
                up_copy(step, p, h).start()

        @pl.when(has_south)
        def _():
            for h in range(CHUNKS):
                down_copy(step, p, h).start()

    def receive(step, p, h):
        @pl.when(has_south)
        def _():
            up_copy(step, p, h).wait_recv()

        @pl.when(has_north)
        def _():
            down_copy(step, p, h).wait_recv()

    def mask_up():
        return pltpu.make_async_remote_copy(
            src_ref=sea_ref, dst_ref=sea_south, send_sem=mask_send.at[0], recv_sem=mask_recv.at[0],
            device_id={"comp": me + 1}, device_id_type=MESH)

    def mask_down():
        return pltpu.make_async_remote_copy(
            src_ref=sea_ref, dst_ref=sea_north, send_sem=mask_send.at[1], recv_sem=mask_recv.at[1],
            device_id={"comp": me - 1}, device_id_type=MESH)

    loads[1].wait()
    pack(0, 0)
    pl.semaphore_wait(barrier, has_south.astype(jnp.int32) + has_north.astype(jnp.int32))

    @pl.when(has_north)
    def _():
        mask_up().start()

    @pl.when(has_south)
    def _():
        mask_down().start()

    send(0, 0)
    loads[2].wait()
    loads[0].wait()
    mat_load = pltpu.make_async_copy(mat_hbm, mat, mat_sem)
    mat_load.start()
    for p in range(1, rows):
        pack(0, p)
        send(0, p)

    @pl.when(jnp.logical_not(has_south))
    def _():
        sea_south[...] = jnp.zeros_like(sea_south)
        south[...] = jnp.zeros_like(south)

    @pl.when(jnp.logical_not(has_north))
    def _():
        sea_north[...] = jnp.zeros_like(sea_north)
        north[...] = jnp.zeros_like(north)

    @pl.when(has_south)
    def _():
        mask_up().wait_recv()

    @pl.when(has_north)
    def _():
        mask_down().wait_recv()

    sea = [sea_ref[pl.ds(r, 1), :].astype(jnp.float32) for r in range(rows)]
    below = [sea_south[pl.ds(rows - 2 + r, 1), :].astype(jnp.float32) for r in range(2)]
    above = [sea_north[pl.ds(1 - r, 1), :].astype(jnp.float32) for r in range(2)]
    thaw = [1.0 - 0.5 * ice_ref[pl.ds(r, 1), :].astype(jnp.float32) for r in range(rows)]
    gain = [RATE * wind_ref[pl.ds(r, 1), :] for r in range(rows)]
    far_up = sea[0] * below[0] * below[1]
    far_down = sea[rows - 1] * above[0] * above[1]

    def courant(d):
        speed = speed_ref[...]
        return speed * trig_ref[pl.ds(d, 1), :], speed * trig_ref[pl.ds(HALF + d, 1), :]

    def advance(step, d, up_shift, down_shift):
        cx, cy = courant(d)
        staying = 1.0 - cx - cy
        halo = pl.ds(pl.multiple_of(d * NFREQ, NFREQ), NFREQ)
        sides = ((south, below + sea, d, up_shift), (north, above + sea[::-1], d + HALF, down_shift))
        for edge, seas, first_row, shift in sides:
            order = list(range(rows)) if edge is south else list(range(rows))[::-1]
            lines = [edge[step, 0, halo, :], edge[step, 1, halo, :]]
            lines += [nat[r, strided(first_row), :] for r in order]
            for s in range(SUBSTEPS):
                moved = []
                for i in range(s, len(lines)):
                    value = staying * lines[i] + cx * pltpu.roll(lines[i], shift, 1)
                    if i > 0:
                        value = value + cy * lines[i - 1]
                    moved.append(seas[i] * value)
                lines = lines[:s] + moved
            for r, line in zip(order, lines[2:]):
                work[r, strided(first_row), :] = line

    def advance_chunk(step, h):
        for start in range(h * PER, (h + 1) * PER, CHUNKS):
            eastward = start < QUARTER
            shifts = (1, width - 1) if eastward else (width - 1, 1)

            def one(i, carry):
                advance(step, start + i, *shifts)
                return carry

            lax.fori_loop(0, CHUNKS, one, 0)

    def far_chunk(step, h):
        def one(i, carry):
            d = h * PER + i
            _, cy = courant(d)
            cube = cy * cy * cy
            halo = pl.ds(pl.multiple_of(d * NFREQ, NFREQ), NFREQ)
            work[0, strided(d), :] += (cube * far_up) * south[step, 2, halo, :]
            work[rows - 1, strided(d + HALF), :] += (cube * far_down) * north[step, 2, halo, :]
            return carry

        lax.fori_loop(0, PER, one, 0)

    def fold(value):
        return jnp.sum(value.reshape(-1, 8, width), axis=0)

    def prepare(which, low):
        for j, r in enumerate(which):
            total[r] = jnp.zeros((8, width), jnp.float32)
            for t in range(K // TILE):
                part = pl.ds(t * TILE, TILE)
                value = work[r, part, :]
                low[0, part, pl.ds(j * width, width)] = value.astype(jnp.bfloat16)
                total[r] += fold(value * value)

    def sources(which, low, finish=None):
        for sub in range(SRC_SUB):
            now, later = sub % 2, (sub + 1) % 2
            last = sub == SRC_SUB - 1
            scale = []
            for r in which:
                energy = jnp.sum(total[r], axis=0, keepdims=True) * (1.0 / K)
                factor = sea[r] / (1.0 + DAMPING * energy)
                scale.append(factor * thaw[r] if last else factor)
                total[r] = jnp.zeros((8, width), jnp.float32)
            for t in range(K // TILE):
                part = pl.ds(t * TILE, TILE)
                growth = jnp.dot(mat[part, :], low[now], preferred_element_type=jnp.float32)
                for j, r in enumerate(which):
                    value = (work[r, part, :] + gain[r] * growth[:, j * width:(j + 1) * width]) * scale[j]
                    if last:
                        nat[r, part, :] = value
                    else:
                        work[r, part, :] = value
                        low[later, part, pl.ds(j * width, width)] = value.astype(jnp.bfloat16)
                        total[r] += fold(value * value)
                if last and finish is not None:
                    finish(t)

    def out_copy(r, t):
        part = pl.ds(t * TILE, TILE)
        return pltpu.make_async_copy(nat.at[r, part], out.at[r, part], out_sem.at[r, t])

    for step in range(STEPS):
        last = step == STEPS - 1
        for h in range(CHUNKS):
            receive(step, 0, h)
            receive(step, 1, h)
            advance_chunk(step, h)
        if step == 0:
            mat_load.wait()
        prepare((1,), low_mid)
        sources((1,), low_mid, (lambda t: out_copy(1, t).start()) if last else None)
        if not last:
            pack(step + 1, 0)
            send(step + 1, 0)
        for h in range(CHUNKS):
            receive(step, 2, h)
            far_chunk(step, h)
        prepare((0, 2), low_out)

        def finish(t):
            out_copy(0, t).start()
            out_copy(2, t).start()

        sources((0, 2), low_out, finish if last else None)
        if not last:
            for p in range(1, rows):
                pack(step + 1, p)
                send(step + 1, p)

    @pl.when(has_north)
    def _():
        mask_up().wait_send()
        for step in range(STEPS):
            for p in range(rows):
                for h in range(CHUNKS):
                    up_copy(step, p, h).wait_send()

    @pl.when(has_south)
    def _():
        mask_down().wait_send()
        for step in range(STEPS):
            for p in range(rows):
                for h in range(CHUNKS):
                    down_copy(step, p, h).wait_send()

    for r in range(rows):
        for t in range(K // TILE):
            out_copy(r, t).wait()


def on_device(spectrum, sea_mask, ice_mask, wind, source_matrix):
    size = lax.axis_size("comp")
    spectra = spectrum.transpose(1, 0, 2)
    rows, _, width = spectra.shape
    speeds, trig = (jnp.asarray(t) for t in tables(width))
    hbm = pl.BlockSpec(memory_space=pl.ANY)
    vmem = pl.BlockSpec(memory_space=pltpu.VMEM)
    dma = pltpu.SemaphoreType.DMA
    full = pltpu.VMEM((rows, K, width), jnp.float32)
    halo = pltpu.VMEM((STEPS, rows, SIDE, width), jnp.float32)
    pieces = dma((STEPS, rows, CHUNKS))
    result = pl.pallas_call(
        functools.partial(kernel, size),
        out_shape=jax.ShapeDtypeStruct(spectra.shape, jnp.float32),
        in_specs=[hbm, vmem, vmem, vmem, hbm, vmem, vmem],
        out_specs=hbm,
        scratch_shapes=[
            full, full, halo, halo, halo, halo,
            pltpu.VMEM(sea_mask.shape, jnp.int32),
            pltpu.VMEM(sea_mask.shape, jnp.int32),
            pltpu.VMEM((K, K), jnp.bfloat16),
            pltpu.VMEM((2, K, width), jnp.bfloat16),
            pltpu.VMEM((2, K, 2 * width), jnp.bfloat16),
            pltpu.VMEM((rows, 8, width), jnp.float32),
            dma((rows,)), dma, dma((2,)), dma((2,)),
            pieces, pieces, pieces, pieces,
            dma((rows, K // TILE)),
        ],
        compiler_params=pltpu.CompilerParams(
            collective_id=0, has_side_effects=True, vmem_limit_bytes=56 * 1024 * 1024),
        name="wave",
    )(spectra, sea_mask, ice_mask, wind, source_matrix, speeds, trig)
    return result.transpose(1, 0, 2)


def solution(mesh):
    return jax.shard_map(
        on_device,
        mesh=mesh,
        in_specs=(
            P(None, ("grp", "comp"), None),
            P(("grp", "comp"), None),
            P(("grp", "comp"), None),
            P(("grp", "comp"), None),
            P(),
        ),
        out_specs=P(None, ("grp", "comp"), None),
        check_vma=False,
    )
```

profile of v0, /device:TPU:1, one launch (start us, length us, event | category | flops | bytes accessed | tf_op | source)
XLA Modules:
  0.0 55.4 jit_solution(8842248384025387548)
XLA Ops:
  0.0 52.6 %wave.1 = f32[3,1152,128]{2,1,0:T(8,128)} custom-call(f32[3,1152,128]{2,1,0:T(8,128)} %bitcast.3, s32[3,128]{1,0:T(4,128)} %sea_ref.1, s32[3,128]{1,0:T(4,128)} %ice_ref.1, f32[3,128]{1,0:T(4,128)} %wind_ref.1, bf16[1152,1152]{1,0:T(8,128)(2,1)} %mat_hbm.1, f32[32,128]{1,0:T(8,128)} %constant.4.clone.speed_ref, f32[36,128]{1,0:T(8,128)} %constant.5.clone.trig_ref), custom_call_target="tpu_custom_call" | custom-call | tf_op jit(solution)/shard_map/wave/pallas_call | solution.py:309
  52.6 2.8 %copy.9 = f32[1152,3,128]{2,0,1:T(8,128)} copy(f32[1152,3,128]{2,0,1:T(8,128)} %bitcast.2) | data formatting | bytes 3538944
where the time goes:
time: 55.7 us; the launch traced here: 55.4 us
  Pallas kernels  52.6 us (94%)
  local copies, waits for them, and re-layouts  2.8 us (5%)
    pallas_call x1, Pallas kernels, on_device(): pl.pallas_call(functools.partial(kernel, size), out_shape=jax.ShapeDtypeS...  52.6 us
    unnamed x1, local copies, waits for them, and re-layouts  2.8 us

commit v1 on v0

--- a/solution.py
+++ b/solution.py
@@ -26,6 +26,9 @@
 TILE = 288
 UP_ROW = (1, 2, 0)
 DOWN_ROW = (1, 0, 2)
+FOLD = 4
+UNITS = 3 * CHUNKS
+RELAYED = 9
 MESH = pl.DeviceIdType.MESH
 
 
@@ -42,12 +45,18 @@
     return pl.ds(d, NFREQ, stride=NDIR)
 
 
-def kernel(size, spec, sea_ref, ice_ref, wind_ref, mat_hbm, speed_ref, trig_ref, out,
+def kernel(size, folded, spec, sea_ref, ice_ref, wind_ref, mat_hbm, speed_ref, trig_ref, out,
            nat, work, south, north, send_up, send_down, sea_south, sea_north, mat, low_mid, low_out,
-           total, load_sem, mat_sem, mask_send, mask_recv, up_send, up_recv, down_send, down_recv, out_sem):
+           total, parcel, load_sem, mat_sem, mask_send, mask_recv, up_send, up_recv, down_send, down_recv, leg_recv, hop_send, out_sem):
     rows, width = spec.shape[0], spec.shape[2]
     me = lax.axis_index("comp")
     has_south, has_north = me > 0, me < size - 1
+    pos, fold_at, folds = me % FOLD, me // FOLD, size // FOLD
+    lower, upper = pos == 0, pos == FOLD - 1
+    later_fold, prior_fold = fold_at < folds - 1, fold_at > 0
+    share_up = (RELAYED * (folds - 1 - fold_at) + folds // 2) // folds
+    share_down = (RELAYED * fold_at + folds // 2) // folds
+    greeted = has_south.astype(jnp.int32) + has_north.astype(jnp.int32)
 
     loads = [pltpu.make_async_copy(spec.at[r], nat.at[r], load_sem.at[r]) for r in range(rows)]
     for r in UP_ROW:
@@ -62,6 +71,60 @@
     @pl.when(has_north)
     def _():
         pl.semaphore_signal(barrier, inc=1, device_id={"comp": me + 1}, device_id_type=MESH)
+
+    if folded:
+        hellos = ((lower, FOLD - 1), (upper, 1 - FOLD))
+        hellos += tuple((jnp.logical_and(end, near), way) for end in (lower, upper)
+                        for near, way in ((later_fold, FOLD), (prior_fold, -FOLD)))
+        for there, way in hellos:
+            @pl.when(there)
+            def _():
+                pl.semaphore_signal(barrier, inc=1, device_id={"comp": me + way}, device_id_type=MESH)
+
+            greeted += there.astype(jnp.int32)
+
+    def relayed(share, p, h):
+        return ((p * CHUNKS + h) * share) % UNITS < share
+
+    def leg(source, step, p, h, send_sem, way):
+        part = pl.ds(h * SPAN, SPAN)
+        return pltpu.make_async_remote_copy(
+            src_ref=source.at[step, p, part], dst_ref=parcel.at[step, p, part],
+            send_sem=send_sem.at[step, p, h], recv_sem=leg_recv.at[step, p, h],
+            device_id={"comp": me + way}, device_id_type=MESH)
+
+    def hop(target, step, p, h, recv_sem, way):
+        part = pl.ds(h * SPAN, SPAN)
+        return pltpu.make_async_remote_copy(
+            src_ref=parcel.at[step, p, part], dst_ref=target.at[step, p, part],
+            send_sem=hop_send.at[step, p, h], recv_sem=recv_sem.at[step, p, h],
+            device_id={"comp": me + way}, device_id_type=MESH)
+
+    def relay(step, p):
+        if not folded:
+            return
+        for h in range(CHUNKS):
+            @pl.when(lower & later_fold & relayed(share_up, p, h))
+            def _():
+                leg(send_up, step, p, h, up_send, 1 - FOLD).wait_recv()
+                hop(south, step, p, h, up_recv, FOLD).start()
+
+            @pl.when(upper & prior_fold & relayed(share_down, p, h))
+            def _():
+                leg(send_down, step, p, h, down_send, FOLD - 1).wait_recv()
+                hop(north, step, p, h, down_recv, -FOLD).start()
+
+    def relay_done(step, p):
+        if not folded:
+            return
+        for h in range(CHUNKS):
+            @pl.when(lower & later_fold & relayed(share_up, p, h))
+            def _():
+                hop(south, step, p, h, up_recv, FOLD).wait_send()
+
+            @pl.when(upper & prior_fold & relayed(share_down, p, h))
+            def _():
+                hop(north, step, p, h, down_recv, -FOLD).wait_send()
 
     def up_copy(step, p, h):
         part = pl.ds(h * SPAN, SPAN)
@@ -83,14 +146,29 @@
             send_down[step, p, pl.ds(d * NFREQ, NFREQ), :] = nat[DOWN_ROW[p], strided(d + HALF), :]
 
     def send(step, p):
-        @pl.when(has_north)
-        def _():
-            for h in range(CHUNKS):
+        for h in range(CHUNKS):
+            by_up, by_down = has_north, has_south
+            if folded:
+                aside = upper & has_north & relayed(share_up, p, h)
+                by_up = has_north & jnp.logical_not(aside)
+
+                @pl.when(aside)
+                def _():
+                    leg(send_up, step, p, h, up_send, 1 - FOLD).start()
+
+                aside = lower & has_south & relayed(share_down, p, h)
+                by_down = has_south & jnp.logical_not(aside)
+
+                @pl.when(aside)
+                def _():
+                    leg(send_down, step, p, h, down_send, FOLD - 1).start()
+
+            @pl.when(by_up)
+            def _():
                 up_copy(step, p, h).start()
 
-        @pl.when(has_south)
-        def _():
-            for h in range(CHUNKS):
+            @pl.when(by_down)
+            def _():
                 down_copy(step, p, h).start()
 
     def receive(step, p, h):
@@ -114,7 +192,7 @@
 
     loads[1].wait()
     pack(0, 0)
-    pl.semaphore_wait(barrier, has_south.astype(jnp.int32) + has_north.astype(jnp.int32))
+    pl.semaphore_wait(barrier, greeted)
 
     @pl.when(has_north)
     def _():
@@ -248,10 +326,13 @@
 
     for step in range(STEPS):
         last = step == STEPS - 1
+        relay(step, 0)
+        relay(step, 1)
         for h in range(CHUNKS):
             receive(step, 0, h)
             receive(step, 1, h)
             advance_chunk(step, h)
+        relay(step, 2)
         if step == 0:
             mat_load.wait()
         prepare((1,), low_mid)
@@ -290,12 +371,16 @@
                 for h in range(CHUNKS):
                     down_copy(step, p, h).wait_send()
 
+    for step in range(STEPS):
+        for p in range(rows):
+            relay_done(step, p)
+
     for r in range(rows):
         for t in range(K // TILE):
             out_copy(r, t).wait()
 
 
-def on_device(spectrum, sea_mask, ice_mask, wind, source_matrix):
+def on_device(folded, spectrum, sea_mask, ice_mask, wind, source_matrix):
     size = lax.axis_size("comp")
     spectra = spectrum.transpose(1, 0, 2)
     rows, _, width = spectra.shape
@@ -307,7 +392,7 @@
     halo = pltpu.VMEM((STEPS, rows, SIDE, width), jnp.float32)
     pieces = dma((STEPS, rows, CHUNKS))
     result = pl.pallas_call(
-        functools.partial(kernel, size),
+        functools.partial(kernel, size, folded),
         out_shape=jax.ShapeDtypeStruct(spectra.shape, jnp.float32),
         in_specs=[hbm, vmem, vmem, vmem, hbm, vmem, vmem],
         out_specs=hbm,
@@ -319,8 +404,9 @@
             pltpu.VMEM((2, K, width), jnp.bfloat16),
             pltpu.VMEM((2, K, 2 * width), jnp.bfloat16),
             pltpu.VMEM((rows, 8, width), jnp.float32),
+            halo,
             dma((rows,)), dma, dma((2,)), dma((2,)),
-            pieces, pieces, pieces, pieces,
+            pieces, pieces, pieces, pieces, pieces, pieces,
             dma((rows, K // TILE)),
         ],
         compiler_params=pltpu.CompilerParams(
@@ -330,9 +416,25 @@
     return result.transpose(1, 0, 2)
 
 
+def is_folded(mesh):
+    line = np.moveaxis(mesh.devices, mesh.axis_names.index("comp"), -1)
+    line = line.reshape(-1, line.shape[-1])[0]
+    places = [getattr(device, "coords", None) for device in line]
+    if len(line) % FOLD or len(line) < 2 * FOLD or None in places:
+        return False
+
+    def hops(a, b):
+        return sum(abs(p - q) for p, q in zip(places[a], places[b]))
+
+    starts = range(0, len(line), FOLD)
+    inside = all([hops(i, i + j) for j in range(FOLD)] == [0, 0, 1, 1] for i in starts)
+    across = all(hops(i - 1, i) == 2 and hops(i - FOLD, i) == 1 for i in starts[1:])
+    return inside and across
+
+
 def solution(mesh):
     return jax.shard_map(
-        on_device,
+        functools.partial(on_device, is_folded(mesh)),
         mesh=mesh,
         in_specs=(
             P(None, ("grp", "comp"), None),

time: 55.7 us -> 50.3 us (0.903)
  Pallas kernels: 52.6 us -> 47.3 us
    pallas_call x1, Pallas kernels: 52.6 us -> 47.3 us  [on_device(): pl.pallas_call(functools.partial(kernel, size, folded), out_shape=jax.Sha...]
where the time goes in v1:
time: 50.3 us; the launch traced here: 50.1 us
  Pallas kernels  47.3 us (94%)
  local copies, waits for them, and re-layouts  2.8 us (6%)
    pallas_call x1, Pallas kernels, on_device(): pl.pallas_call(functools.partial(kernel, size, folded), out_shape=jax.Sha...  47.3 us
    unnamed x1, local copies, waits for them, and re-layouts  2.8 us

profile of v1, /device:TPU:1, one launch (start us, length us, event | category | flops | bytes accessed | tf_op | source)
XLA Modules:
  0.0 50.1 jit_solution(16022577071049169509)
XLA Ops:
  0.0 47.3 %wave.1 = f32[3,1152,128]{2,1,0:T(8,128)} custom-call(f32[3,1152,128]{2,1,0:T(8,128)} %bitcast.3, s32[3,128]{1,0:T(4,128)} %sea_ref.1, s32[3,128]{1,0:T(4,128)} %ice_ref.1, f32[3,128]{1,0:T(4,128)} %wind_ref.1, bf16[1152,1152]{1,0:T(8,128)(2,1)} %mat_hbm.1, f32[32,128]{1,0:T(8,128)} %constant.4.clone.speed_ref, f32[36,128]{1,0:T(8,128)} %constant.5.clone.trig_ref), custom_call_target="tpu_custom_call" | custom-call | tf_op jit(solution)/shard_map/wave/pallas_call | solution.py:394
  47.3 2.8 %copy.9 = f32[1152,3,128]{2,0,1:T(8,128)} copy(f32[1152,3,128]{2,0,1:T(8,128)} %bitcast.2) | data formatting | bytes 3538944

commit v2 on v1

--- a/solution.py
+++ b/solution.py
@@ -47,7 +47,7 @@
 
 def kernel(size, folded, spec, sea_ref, ice_ref, wind_ref, mat_hbm, speed_ref, trig_ref, out,
            nat, work, south, north, send_up, send_down, sea_south, sea_north, mat, low_mid, low_out,
-           total, parcel, load_sem, mat_sem, mask_send, mask_recv, up_send, up_recv, down_send, down_recv, leg_recv, hop_send, out_sem):
+           total, parcel, load_sem, mat_sem, mask_send, mask_recv, up_send, up_recv, down_send, down_recv, leg_recv, hop_send):
     rows, width = spec.shape[0], spec.shape[2]
     me = lax.axis_index("comp")
     has_south, has_north = me > 0, me < size - 1
@@ -296,7 +296,7 @@
                 low[0, part, pl.ds(j * width, width)] = value.astype(jnp.bfloat16)
                 total[r] += fold(value * value)
 
-    def sources(which, low, finish=None):
+    def sources(which, low, result):
         for sub in range(SRC_SUB):
             now, later = sub % 2, (sub + 1) % 2
             last = sub == SRC_SUB - 1
@@ -312,17 +312,11 @@
                 for j, r in enumerate(which):
                     value = (work[r, part, :] + gain[r] * growth[:, j * width:(j + 1) * width]) * scale[j]
                     if last:
-                        nat[r, part, :] = value
+                        result[r, part, :] = value
                     else:
                         work[r, part, :] = value
                         low[later, part, pl.ds(j * width, width)] = value.astype(jnp.bfloat16)
                         total[r] += fold(value * value)
-                if last and finish is not None:
-                    finish(t)
-
-    def out_copy(r, t):
-        part = pl.ds(t * TILE, TILE)
-        return pltpu.make_async_copy(nat.at[r, part], out.at[r, part], out_sem.at[r, t])
 
     for step in range(STEPS):
         last = step == STEPS - 1
@@ -336,7 +330,8 @@
         if step == 0:
             mat_load.wait()
         prepare((1,), low_mid)
-        sources((1,), low_mid, (lambda t: out_copy(1, t).start()) if last else None)
+        result = out if last else nat
+        sources((1,), low_mid, result)
         if not last:
             pack(step + 1, 0)
             send(step + 1, 0)
@@ -345,11 +340,7 @@
             far_chunk(step, h)
         prepare((0, 2), low_out)
 
-        def finish(t):
-            out_copy(0, t).start()
-            out_copy(2, t).start()
-
-        sources((0, 2), low_out, finish if last else None)
+        sources((0, 2), low_out, result)
         if not last:
             for p in range(1, rows):
                 pack(step + 1, p)
@@ -374,10 +365,6 @@
     for step in range(STEPS):
         for p in range(rows):
             relay_done(step, p)
-
-    for r in range(rows):
-        for t in range(K // TILE):
-            out_copy(r, t).wait()
 
 
 def on_device(folded, spectrum, sea_mask, ice_mask, wind, source_matrix):
@@ -391,11 +378,11 @@
     full = pltpu.VMEM((rows, K, width), jnp.float32)
     halo = pltpu.VMEM((STEPS, rows, SIDE, width), jnp.float32)
     pieces = dma((STEPS, rows, CHUNKS))
-    result = pl.pallas_call(
+    state = pl.pallas_call(
         functools.partial(kernel, size, folded),
-        out_shape=jax.ShapeDtypeStruct(spectra.shape, jnp.float32),
+        out_shape=pltpu.VMEM(spectra.shape, jnp.float32),
         in_specs=[hbm, vmem, vmem, vmem, hbm, vmem, vmem],
-        out_specs=hbm,
+        out_specs=vmem,
         scratch_shapes=[
             full, full, halo, halo, halo, halo,
             pltpu.VMEM(sea_mask.shape, jnp.int32),
@@ -407,13 +394,12 @@
             halo,
             dma((rows,)), dma, dma((2,)), dma((2,)),
             pieces, pieces, pieces, pieces, pieces, pieces,
-            dma((rows, K // TILE)),
         ],
         compiler_params=pltpu.CompilerParams(
-            collective_id=0, has_side_effects=True, vmem_limit_bytes=56 * 1024 * 1024),
+            collective_id=0, has_side_effects=True, vmem_limit_bytes=58 * 1024 * 1024),
         name="wave",
     )(spectra, sea_mask, ice_mask, wind, source_matrix, speeds, trig)
-    return result.transpose(1, 0, 2)
+    return state.transpose(1, 0, 2)
 
 
 def is_folded(mesh):

time: 50.3 us -> 47.9 us (0.952)
  local copies, waits for them, and re-layouts: 2.8 us -> 1.21 us
  Pallas kernels: 47.3 us -> 46.5 us
    unnamed x1, local copies, waits for them, and re-layouts: 2.8 us -> 1.21 us
    pallas_call x1, Pallas kernels: 47.3 us -> 46.5 us  [on_device(): pl.pallas_call(functools.partial(kernel, size, folded), out_shape=pltpu.V...]
where the time goes in v2:
time: 47.9 us; the launch traced here: 47.7 us
  Pallas kernels  46.5 us (97%)
  local copies, waits for them, and re-layouts  1.21 us (3%)
    pallas_call x1, Pallas kernels, on_device(): pl.pallas_call(functools.partial(kernel, size, folded), out_shape=pltpu.V...  46.5 us
    unnamed x1, local copies, waits for them, and re-layouts  1.21 us

profile of v2, /device:TPU:1, one launch (start us, length us, event | category | flops | bytes accessed | tf_op | source)
XLA Modules:
  0.0 47.7 jit_solution(9297810895521729257)
XLA Ops:
  0.0 46.5 %wave.1 = f32[3,1152,128]{2,1,0:T(8,128)S(1)} custom-call(f32[3,1152,128]{2,1,0:T(8,128)} %bitcast.3, s32[3,128]{1,0:T(4,128)} %sea_ref.1, s32[3,128]{1,0:T(4,128)} %ice_ref.1, f32[3,128]{1,0:T(4,128)} %wind_ref.1, bf16[1152,1152]{1,0:T(8,128)(2,1)} %mat_hbm.1, f32[32,128]{1,0:T(8,128)} %constant.4.clone.speed_ref, f32[36,128]{1,0:T(8,128)} %constant.5.clone.trig_ref), custom_call_target="tpu_custom_call" | custom-call | tf_op jit(solution)/shard_map/wave/pallas_call | solution.py:381
  46.5 1.2 %copy.9 = f32[1152,3,128]{2,0,1:T(8,128)} copy(f32[1152,3,128]{2,0,1:T(8,128)S(1)} %bitcast.2) | data formatting | bytes 3538944

commit v3 on v2

--- a/solution.py
+++ b/solution.py
@@ -20,15 +20,16 @@
 HALF = NDIR // 2
 QUARTER = HALF // 2
 SIDE = HALF * NFREQ
-CHUNKS = 3
+CHUNKS = 6
 PER = HALF // CHUNKS
 SPAN = PER * NFREQ
 TILE = 288
+BATCH = 3
 UP_ROW = (1, 2, 0)
 DOWN_ROW = (1, 0, 2)
 FOLD = 4
 UNITS = 3 * CHUNKS
-RELAYED = 9
+RELAYED = 16
 MESH = pl.DeviceIdType.MESH
 
 
@@ -84,7 +85,7 @@
             greeted += there.astype(jnp.int32)
 
     def relayed(share, p, h):
-        return ((p * CHUNKS + h) * share) % UNITS < share
+        return p * CHUNKS + h >= UNITS - share
 
     def leg(source, step, p, h, send_sem, way):
         part = pl.ds(h * SPAN, SPAN)
@@ -262,7 +263,7 @@
                 work[r, strided(first_row), :] = line
 
     def advance_chunk(step, h):
-        for start in range(h * PER, (h + 1) * PER, CHUNKS):
+        for start in range(h * PER, (h + 1) * PER, BATCH):
             eastward = start < QUARTER
             shifts = (1, width - 1) if eastward else (width - 1, 1)
 
@@ -270,7 +271,7 @@
                 advance(step, start + i, *shifts)
                 return carry
 
-            lax.fori_loop(0, CHUNKS, one, 0)
+            lax.fori_loop(0, BATCH, one, 0)
 
     def far_chunk(step, h):
         def one(i, carry):

time: 47.9 us -> 47.8 us (level)
  no operation moved by 1% of the time
where the time goes in v3:
time: 47.8 us; the launch traced here: 47.6 us
  Pallas kernels  46.4 us (97%)
  local copies, waits for them, and re-layouts  1.21 us (3%)
    pallas_call x1, Pallas kernels, on_device(): pl.pallas_call(functools.partial(kernel, size, folded), out_shape=pltpu.V...  46.4 us
    unnamed x1, local copies, waits for them, and re-layouts  1.21 us

profile of v3, /device:TPU:1, one launch (start us, length us, event | category | flops | bytes accessed | tf_op | source)
XLA Modules:
  0.0 47.6 jit_solution(13266914216218781060)
XLA Ops:
  0.0 46.4 %wave.1 = f32[3,1152,128]{2,1,0:T(8,128)S(1)} custom-call(f32[3,1152,128]{2,1,0:T(8,128)} %bitcast.3, s32[3,128]{1,0:T(4,128)} %sea_ref.1, s32[3,128]{1,0:T(4,128)} %ice_ref.1, f32[3,128]{1,0:T(4,128)} %wind_ref.1, bf16[1152,1152]{1,0:T(8,128)(2,1)} %mat_hbm.1, f32[32,128]{1,0:T(8,128)} %constant.4.clone.speed_ref, f32[36,128]{1,0:T(8,128)} %constant.5.clone.trig_ref), custom_call_target="tpu_custom_call" | custom-call | tf_op jit(solution)/shard_map/wave/pallas_call | solution.py:382
  46.4 1.2 %copy.9 = f32[1152,3,128]{2,0,1:T(8,128)} copy(f32[1152,3,128]{2,0,1:T(8,128)S(1)} %bitcast.2) | data formatting | bytes 3538944
